TPU v7x, 512 devices: a whole 4x8x8 slice. The times are simulated.
512 devices in a mesh: row: 8 (over y), col: 16 (over x, z_hi, core), layer: 4 (over z_lo).
Axes of the slice: x: 4, y: 8, z: 8 (z_hi: 2, z_lo: 4; z = z_hi * 4 + z_lo), core: 2. Of those that a mesh axis runs over, the one named last changes fastest.
Arguments:
- sign_iterate: bfloat16 [8192, 8192], P('row', 'col'), may hold values from -0.109375 to 0.109375
- square: bfloat16 [8192, 8192], P('row', 'col'), may hold values from -6 to 6
- pattern: int32 [64, 64], replicated, may hold values 0 or 1
- keep: int32 [64, 64], replicated, may hold values from 0 to 1, as said below
Outputs:
- product: bfloat16 [8192, 8192], P(('row', 'layer'), 'col')
Inputs may be any that keep to these rules, and one draw needn't show every extreme that they name: In every region of 2 block rows by 4 block columns, aligned to the output's shards along row+layer and col, exactly 6 blocks have keep 1.
All inputs are finite; a program needn't handle non-finite values.
Results may differ from a plain program's by a relative error of at most 0.001.
Values may be sent and summed in bfloat16 or wider, within the bound.
No kernel may reach another device: no remote copies, remote signals or barrier semaphores. Data moves between devices by JAX's collectives and lax.ppermute only.
A program may use at most 64 MiB of HBM per device.

v0:
```python
import jax
import jax.numpy as jnp
from jax import lax
from jax.sharding import PartitionSpec as P

BLK = 128


def apply_blocks(matrix, mask):
    nrow = mask.shape[0]
    ncol = mask.shape[1]
    shaped = matrix.reshape(nrow, BLK, ncol, BLK)
    chosen = (mask == 1)[:, None, :, None]
    return jnp.where(chosen, shaped, jnp.zeros_like(shaped)).reshape(matrix.shape)


def shards(sign_iterate, square, pattern, keep):
    layers = lax.axis_size("layer")
    layer_idx = lax.axis_index("layer")
    row_idx = lax.axis_index("row")
    col_idx = lax.axis_index("col")
    rows, cols = sign_iterate.shape
    span = cols // layers
    own_cols = lax.dynamic_slice_in_dim(sign_iterate, layer_idx * span, span, 1)
    first_col = (col_idx * layers + layer_idx) * (span // BLK)
    own_mask = lax.dynamic_slice(
        pattern, (row_idx * (rows // BLK), first_col), (rows // BLK, span // BLK)
    )
    stored = apply_blocks(own_cols, own_mask)
    sq_rows, sq_cols = square.shape
    groups = sq_rows // (span * layers)
    shaped = square.reshape(groups, layers, span, sq_cols)
    own_rows = lax.dynamic_index_in_dim(shaped, layer_idx, 1, False).reshape(groups * span, sq_cols)
    square_all = lax.all_gather(own_rows, "row", axis=0, tiled=True)
    partial_value = jnp.dot(
        lax.all_gather(stored, "col", axis=1, tiled=True),
        square_all,
        preferred_element_type=jnp.float32,
    )
    out_rows = rows // layers
    region_rows = out_rows // BLK
    region_cols = sq_cols // BLK
    first_row = (row_idx * layers + layer_idx) * region_rows
    keep_here = lax.dynamic_slice(
        keep, (first_row, col_idx * region_cols), (region_rows, region_cols)
    )
    summed = lax.psum_scatter(partial_value, "layer", scatter_dimension=0, tiled=True)
    return apply_blocks(summed, keep_here).astype(jnp.bfloat16)


def solution(mesh):
    return jax.shard_map(
        shards,
        mesh=mesh,
        in_specs=(P("row", "col"), P("row", "col"), P(), P()),
        out_specs=P(("row", "layer"), "col"),
        check_vma=False,
    )
```

profile of v0, /device:TPU:1, one launch (start us, length us, event | category | flops | bytes accessed | tf_op | source)
XLA Modules:
  0.0 206.6 jit_solution(8617208817056908263)
XLA Ops:
  6.5 0.0 copy-start
  6.5 0.0 all-gather.5.cloned.1.call-start
  6.5 1.2 copy-done
  7.8 0.7 constant_dynamic-slice_fusion
  8.5 0.0 all-gather.5.cloned.1.call-update
  8.5 0.0 all-gather.3.cloned.1.call-start
  8.6 0.9 fusion
  9.4 0.1 broadcast_bitcast_fusion
  9.5 1.9 dynamic-slice_select_fusion
  11.4 0.0 all-gather.3.cloned.1.call-update
  11.4 0.0 reduce-scatter.2.cloned.1.call-start
  11.5 42.7 %all-gather.5.cloned.1.call-done = bf16[2048,512]{1,0:T(8,128)(2,1)} async-done(((bf16[256,512]{1,0:T(8,128)(2,1)}), bf16[2048,512]{1,0:T(8,128)(2,1)}) %all-gather.5.cloned.1.call-update) | async-done | bytes 2097168 | tf_op jit(solution)/shard_map/all_gather | solution.py:34
  54.1 90.1 %all-gather.3.cloned.1.call-done = bf16[1024,2048]{1,0:T(8,128)(2,1)} async-done(((bf16[1024,128]{1,0:T(8,128)(2,1)}), bf16[1024,2048]{1,0:T(8,128)(2,1)}) %all-gather.3.cloned.1.call-update) | async-done | bytes 4194320 | tf_op jit(solution)/shard_map/all_gather | solution.py:36
  144.2 6.5 %fusion.1 = f32[1024,512]{1,0:T(8,128)} fusion(bf16[1024,2048]{1,0:T(8,128)(2,1)} %all-gather.3.cloned.1.call-done, bf16[2048,512]{1,0:T(8,128)(2,1)} %all-gather.5.cloned.1.call-done), kind=kOutput, calls=%fused_computation.7 | convolution fusion | flops 2147483648 | bytes 8388608 | tf_op jit(solution)/shard_map/dot_general | solution.py:35
  150.7 0.0 reduce-scatter.2.cloned.1.call-update
  150.8 0.8 dynamic-slice_compare_fusion.1
  151.5 46.6 %reduce-scatter.2.cloned.1.call-done = f32[256,512]{1,0:T(8,128)} async-done(((f32[1024,512]{1,0:T(8,128)}), f32[256,512]{1,0:T(8,128)}) %reduce-scatter.2.cloned.1.call-update) | async-done | bytes 524304 | tf_op jit(solution)/shard_map/reduce_scatter | solution.py:47
  198.1 0.1 broadcast_in_dim.32
  198.2 1.8 select_convert_fusion
Async XLA Ops:
  6.5 1.2 copy-start
  6.5 47.6 %all-gather.5.cloned.1.call-start = ((), (), s32[]{:S(2)}) async-start(), calls=%async_computation.2 | async-start | bytes 2359296 | tf_op jit(solution)/shard_map/all_gather | solution.py:34
  8.5 135.7 %all-gather.3.cloned.1.call-start = ((), (), s32[]{:S(2)}) async-start(), calls=%async_computation.1 | async-start | bytes 4456448 | tf_op jit(solution)/shard_map/all_gather | solution.py:36
  11.4 186.7 %reduce-scatter.2.cloned.1.call-start = ((), (), s32[]{:S(2)}) async-start(), calls=%async_computation.3 | async-start | bytes 2621440 | tf_op jit(solution)/shard_map/reduce_scatter | solution.py:47
Sparse Core Ops, SparseCore 0:
  9.4 44.6 all-gather.4
  57.2 86.9 all-gather.2
  150.9 47.1 reduce-scatter.1
where the time goes:
time: 207 us
  waiting for transfers between devices  179 us (86%)
  between operations  13.1 us (6%)
  matrix products  6.53 us (3%)
  other arithmetic  5.34 us (3%)
  local copies, waits for them, and re-layouts  2.16 us (1%)
    all_gather x1, waiting for transfers between devices, shards(): lax.all_gather(stored, 'col', axis=1, tiled=True)  90.1 us
    reduce_scatter x1, waiting for transfers between devices, shards(): lax.psum_scatter(partial_value, 'layer', scatter_dimension=0, tiled=True)  46.6 us
    all_gather x1, waiting for transfers between devices, shards(): square_all = lax.all_gather(own_rows, 'row', axis=0, tiled=True)  42.7 us
    dot_general x1, matrix products, shards(): jnp.dot(lax.all_gather(stored, 'col', axis=1, tiled=True), square_all, pr...  6.53 us
  transfers between devices with their start and end apart: 3, of which 3 were waited for; matrix products, arithmetic and copies ran while one was open for 2% of the time, Pallas kernels for 0%

commit v1 on v0

v1 whole, which is shorter than its diff:
```python
import functools

import jax
import jax.numpy as jnp
from jax import lax
from jax.experimental import pallas as pl
from jax.experimental.pallas import tpu as pltpu
from jax.sharding import PartitionSpec as P


BLK = 128
AXES = ("row", "col", "layer")
ROWS, XS, LAYERS = 8, 4, 4
KEPT = 6


def table(move):
    pairs = []
    for r in range(ROWS):
        for x in range(XS):
            for z in range(2):
                for k in range(2):
                    for l in range(LAYERS):
                        r2, x2, z2, k2, l2 = move(r, x, z, k, l)
                        here = (r * 16 + x * 4 + z * 2 + k) * LAYERS + l
                        there = ((r2 % ROWS) * 16 + (x2 % XS) * 4 + z2 * 2 + k2) * LAYERS + l2
                        pairs.append((here, there))
    return pairs


ALONG_X = table(lambda r, x, z, k, l: (r, x + 1 - 2 * k, z, k, l))
ACROSS_Z = table(lambda r, x, z, k, l: (r, x, 1 - z, k, l ^ 2))
OTHER_CORE = table(lambda r, x, z, k, l: (r, x, z, 1 - k, l))
CORE_PAIRS = [[2 * i, 2 * i + 1] for i in range(8)]


def both_cores(value):
    return lax.all_gather(value, "col", axis=0, tiled=False, axis_index_groups=CORE_PAIRS)


SMEM = pl.BlockSpec(memory_space=pltpu.SMEM)
VMEM = pl.BlockSpec(memory_space=pltpu.VMEM)


def place(xs_ref, column, slab, row, first, lines, pattern_ref, at_ref):
    y, l = at_ref[0], at_ref[4]
    for g in range(2):
        for b in range(2):
            spot = pl.ds(pl.multiple_of(column + g * 2 * BLK + b * BLK, BLK), BLK)
            which = row * 8 + g * 4 + lax.rem(l, 2) * 2 + b
            for i in range(lines):
                source = pl.ds(pl.multiple_of((first + i) * BLK, BLK), BLK)
                part = slab[g, source, b * BLK:(b + 1) * BLK]
                stored = pattern_ref[y * 8 + lax.div(l, 2) * 4 + first + i, which] == 1
                xs_ref[i * BLK:(i + 1) * BLK, spot] = jnp.where(stored, part, jnp.zeros_like(part))


def opposite(at_ref, zsel):
    row = 2 * lax.rem(at_ref[1] + 2, XS) + lax.rem(at_ref[2] + zsel, 2)
    return row, lax.rem(row - at_ref[0] + 8, ROWS)


def early_kernel(at_ref, pattern_ref, *refs):
    slabs, pieces, (out_ref, last_ref, xs4_ref, xs_ref, x_ref, s_ref, sems) = refs[:3], refs[3:10], refs[10:]
    y, x, z, k = (at_ref[i] for i in range(4))
    d = 1 - 2 * k
    copies = [pltpu.make_async_copy(slab, x_ref.at[i], sems.at[i]) for i, slab in enumerate(slabs)]
    copies += [pltpu.make_async_copy(piece, s_ref.at[i], sems.at[3 + i]) for i, piece in enumerate(pieces)]
    for copy in copies:
        copy.start()

    def position(step):
        return jnp.where(step < 4, step, jnp.where(step == 4, 7, step - 1))

    for i, x_at in enumerate((x, x - d, x + d)):
        copies[i].wait()
        for zsel in range(2):
            row = 2 * lax.rem(x_at + 8, XS) + lax.rem(z + zsel, 2)
            column = position(lax.rem(row - y + 8, ROWS)) * 4 * BLK
            place(xs_ref, column, x_ref.at[i, zsel], row, 0, 4, pattern_ref, at_ref)
    for copy in copies[3:]:
        copy.wait()
    for zsel in range(2):
        at = position(opposite(at_ref, zsel)[1])
        xs_ref[:, pl.ds(pl.multiple_of(at * 4 * BLK, BLK), 4 * BLK)] = jnp.zeros((512, 4 * BLK), jnp.bfloat16)
        last_ref[zsel] = s_ref[jnp.minimum(at, 6)]
    xs4_ref[...] = xs_ref[:, 28 * BLK:]
    for i in range(2):
        lines = slice(i * 2 * BLK, (i + 1) * 2 * BLK)
        right = s_ref[...].reshape(28 * BLK, 512)
        out_ref[lines, :] = jnp.dot(xs_ref[lines, :28 * BLK], right, preferred_element_type=jnp.float32)


def early(at, pattern, slabs, pieces):
    return pl.pallas_call(
        early_kernel,
        out_shape=(
            jax.ShapeDtypeStruct((512, 512), jnp.float32),
            jax.ShapeDtypeStruct((2, 512, 512), jnp.bfloat16),
            jax.ShapeDtypeStruct((512, 512), jnp.bfloat16),
        ),
        in_specs=[SMEM] * 2 + [pl.BlockSpec(memory_space=pltpu.HBM)] * 10,
        out_specs=(VMEM,) * 3,
        scratch_shapes=[
            pltpu.VMEM((512, 4096), jnp.bfloat16),
            pltpu.VMEM((3, 2, 2, 512, 256), jnp.bfloat16),
            pltpu.VMEM((7, 512, 512), jnp.bfloat16),
            pltpu.SemaphoreType.DMA((10,)),
        ],
        compiler_params=pltpu.CompilerParams(vmem_limit_bytes=16 * 2**20),
        cost_estimate=pl.CostEstimate(flops=2 * 512 * 4096 * 512, bytes_accessed=4 * 2**20, transcendentals=0),
        name="early",
    )(at, pattern, *slabs, *pieces)


def kept(keep_ref, at_ref, region):
    y, c = at_ref[0], at_ref[5]
    flags = [keep_ref[y * 8 + region * 2 + a, c * 4 + b] == 1 for a in range(2) for b in range(4)]
    spots, at = [], jnp.int32(0)
    for flag in flags:
        spots.append(pl.ds(pl.multiple_of(jnp.minimum(at, KEPT - 1) * BLK, BLK), BLK))
        at = at + flag.astype(jnp.int32)
    return flags, spots


def late_kernel(shift, at_ref, pattern_ref, keep_ref, x2_ref, s4a_ref, s4b_ref, last_ref, xs4_ref, sum_ref, out_ref, xs_ref):
    l = at_ref[4]
    part = lax.rem(l + shift, 2)
    lines = pl.ds(pl.multiple_of(part * 2 * BLK, 2 * BLK), 2 * BLK)
    xs_ref[:, :8 * BLK] = jnp.zeros((2 * BLK, 8 * BLK), jnp.bfloat16)
    xs_ref[:, 8 * BLK:] = xs4_ref[lines, :]
    for zsel in range(2):
        row, step = opposite(at_ref, zsel)
        column = jnp.where(step == 4, 2, zsel) * 4 * BLK
        place(xs_ref, column, x2_ref.at[zsel], row, part * 2, 2, pattern_ref, at_ref)
    right = jnp.concatenate([last_ref[0], last_ref[1], s4a_ref[...], s4b_ref[...]], axis=0)
    value = sum_ref[lines, :] + jnp.dot(xs_ref[...], right, preferred_element_type=jnp.float32)
    flags, spots = kept(keep_ref, at_ref, lax.div(l, 2) * 2 + part)
    for i, (flag, spot) in enumerate(zip(flags, spots)):
        a, b = i // 4, i % 4

        @pl.when(flag)
        def _():
            out_ref[spot, :] = value[a * BLK:(a + 1) * BLK, b * BLK:(b + 1) * BLK]


def late(shift, at, pattern, keep, *arrays):
    return pl.pallas_call(
        functools.partial(late_kernel, shift),
        out_shape=jax.ShapeDtypeStruct((KEPT * BLK, BLK), jnp.float32),
        in_specs=[SMEM] * 3 + [VMEM] * 6,
        out_specs=VMEM,
        scratch_shapes=[pltpu.VMEM((2 * BLK, 12 * BLK), jnp.bfloat16)],
        compiler_params=pltpu.CompilerParams(vmem_limit_bytes=12 * 2**20),
        cost_estimate=pl.CostEstimate(flops=2 * 256 * 1536 * 512, bytes_accessed=2**20, transcendentals=0),
    )(at, pattern, keep, *arrays)


def finish_kernel(at_ref, keep_ref, own_ref, got_ref, out_ref):
    flags, spots = kept(keep_ref, at_ref, at_ref[4])
    for i, (flag, spot) in enumerate(zip(flags, spots)):
        a, b = i // 4, i % 4
        total = jnp.where(flag, own_ref[spot, :] + got_ref[spot, :], 0.0)
        out_ref[a * BLK:(a + 1) * BLK, b * BLK:(b + 1) * BLK] = total.astype(jnp.bfloat16)


def finish(at, keep, own, got):
    return pl.pallas_call(
        finish_kernel,
        out_shape=jax.ShapeDtypeStruct((2 * BLK, 4 * BLK), jnp.bfloat16),
        in_specs=[SMEM, SMEM, VMEM, VMEM],
        out_specs=VMEM,
        compiler_params=pltpu.CompilerParams(vmem_limit_bytes=8 * 2**20),
        cost_estimate=pl.CostEstimate(flops=2**20, bytes_accessed=2 * 2**20, transcendentals=0),
        name="finish",
    )(at, keep, own, got)


def body(sign_iterate, square, pattern, keep):
    l = lax.axis_index("layer")
    y = lax.axis_index("row")
    c = lax.axis_index("col")
    half, part = l // 2, l % 2
    at = jnp.stack([y, c // 4, (c // 2) % 2, c % 2, l, c]).astype(jnp.int32)
    at, sign_iterate, square = lax.optimization_barrier((at, sign_iterate, square))

    def step(value, pairs):
        return lax.ppermute(value, AXES, pairs)

    def down(value, shift):
        return step(value, table(lambda r, x, z, k, l: (r + shift, x, z, k, l)))

    def slab(rows):
        return lax.dynamic_slice(sign_iterate, (rows * 512, part * 256), (512, 256))

    z_own = step(slab(1 - half), ACROSS_Z)
    s0 = lax.dynamic_index_in_dim(square.reshape(2, 2, 256, 512), part, 1, False).reshape(512, 512)
    s7 = down(s0, 1)
    s1 = down(s0, -1)
    x0 = jnp.stack([both_cores(slab(half)), both_cores(z_own)])
    x1 = step(x0, ALONG_X)
    s6 = down(s7, 1)
    s2 = down(s1, -1)
    s5 = down(s6, 1)
    s3 = down(s2, -1)
    x2 = step(x1, ALONG_X)
    x1o = step(x1, OTHER_CORE)
    s4a = down(s5[:256], 1)
    s4b = down(s3[256:], -1)
    total, last, xs4 = early(at, pattern, (x0, x1, x1o), (s0, s1, s2, s3, s5, s6, s7))
    rest = (x2, s4a, s4b, last, xs4, total)
    sent = late(1, at, pattern, keep, *rest)
    got = step(sent, table(lambda r, x, z, k, l: (r, x, z, k, l ^ 1)))
    own = late(0, at, pattern, keep, *rest)
    return finish(at, keep, own, got)


def solution(mesh):
    return jax.shard_map(
        body,
        mesh=mesh,
        in_specs=(P("row", "col"), P("row", "col"), P(), P()),
        out_specs=P(("row", "layer"), "col"),
        check_vma=False,
    )
```

time: 207 us -> 109 us (0.53)
  the two profiles are of different devices: /device:TPU:1 before, /device:TPU:64 now
where the time goes in v1:
time: 109 us
  starting transfers between devices  49 us (45%)
  waiting for transfers between devices  42.1 us (39%)
  Pallas kernels  11.8 us (11%)
  blocking collectives  4.35 us (4%)
  local copies, waits for them, and re-layouts  1.32 us (1%)
    ppermute x13, starting transfers between devices, step(): return lax.ppermute(value, AXES, pairs)  49 us
    ppermute x13, waiting for transfers between devices, step(): return lax.ppermute(value, AXES, pairs)  42.1 us
    pallas_call x1, Pallas kernels, early(): pl.pallas_call(early_kernel, out_shape=(jax.ShapeDtypeStruct((512, 512),...  5.24 us
    pallas_call x2, Pallas kernels, late(): pl.pallas_call(functools.partial(late_kernel, shift), out_shape=jax.Shape...  4.68 us
    all_gather x2, blocking collectives, both_cores(): lax.all_gather(value, 'col', axis=0, tiled=False, axis_index_groups=CORE_...  4.35 us
  transfers between devices with their start and end apart: 13, of which 6 were waited for; matrix products, arithmetic and copies ran while one was open for 0% of the time, Pallas kernels for 7%

profile of v1, /device:TPU:64, one launch (start us, length us, event | category | flops | bytes accessed | tf_op | source)
XLA Modules:
  0.0 108.9 jit_solution(4122671249552368131)
XLA Ops:
  0.0 0.0 copy-start
  0.0 0.1 stack.36.at_ref
  0.1 1.1 %fusion = (bf16[512,256]{1,0:T(8,128)(2,1)S(1)}, bf16[512,256]{1,0:T(8,128)(2,1)S(1)}) fusion(bf16[1024,512]{1,0:T(8,128)(2,1)} %param.4, s32[]{:T(128)S(6)} %select_n.44, s32[]{:T(128)S(6)} %select_n.46, s32[]{:T(128)S(6)} %select_n.47), kind=kLoop, calls=%fused_computation.2 | loop fusion | bytes 1048588 | tf_op jit(solution)/shard_map/dynamic_slice | solution.py:194
  1.2 10.0 %collective-permute-start = (bf16[512,256]{1,0:T(8,128)(2,1)S(1)}, bf16[512,256]{1,0:T(8,128)(2,1)S(1)}, u32[]{:S(2)}, u32[]{:S(2)}) collective-permute-start(bf16[512,256]{1,0:T(8,128)(2,1)S(1)} %get-tuple-element.18), channel_id=1, source_target_pairs={{0,10},{1,11},{2,8},{3,9},{4,14},{5,15},{6,12},{7,13},{8,2},{9,3},... | collective-permute-start | bytes 786440 | tf_op jit(solution)/shard_map/ppermute | solution.py:188
  11.3 2.2 %all-gather = bf16[1024,256]{1,0:T(8,128)(2,1)S(1)} all-gather(bf16[512,256]{1,0:T(8,128)(2,1)S(1)} %get-tuple-element.17), channel_id=2, replica_groups={{0,4},{8,12},{16,20},{24,28},{32,36},{40,44},{48,52},{56,60},{1,5},{9,1..., dimensions={0}, use_global_device_ids=true | all-gather | bytes 786432 | tf_op jit(solution)/shard_map/all_gather | solution.py:38
  13.5 9.7 %collective-permute-done = bf16[512,256]{1,0:T(8,128)(2,1)S(1)} collective-permute-done((bf16[512,256]{1,0:T(8,128)(2,1)S(1)}, bf16[512,256]{1,0:T(8,128)(2,1)S(1)}, u32[]{:S(2)}, u32[]{:S(2)}) %collective-permute-start) | collective-permute-done | bytes 262176 | tf_op jit(solution)/shard_map/ppermute | solution.py:188
  23.2 2.2 %all-gather.1 = bf16[1024,256]{1,0:T(8,128)(2,1)S(1)} all-gather(bf16[512,256]{1,0:T(8,128)(2,1)S(1)} %collective-permute-done), channel_id=3, replica_groups={{0,4},{8,12},{16,20},{24,28},{32,36},{40,44},{48,52},{56,60},{1,5},{9,1..., dimensions={0}, use_global_device_ids=true | all-gather | bytes 786432 | tf_op jit(solution)/shard_map/all_gather | solution.py:38
  25.3 0.1 pad_maximum_fusion.refs_0_
  25.4 3.4 %collective-permute-start.1 = (bf16[2,2,512,256]{3,2,1,0:T(8,128)(2,1)S(1)}, bf16[2,2,512,256]{3,2,1,0:T(8,128)(2,1)S(1)}, u32[]{:S(2)}, u32[]{:S(2)}) collective-permute-start(bf16[2,2,512,256]{3,2,1,0:T(8,128)(2,1)S(1)} %pad_maximum_fusion.refs_0_), channel_id=1, source_target_pairs={{0,16},{1,17},{2,18},{3,19},{4,52},{5,53},{6,54},{7,55},{8,24},{9,... | collective-permute-start | bytes 3145736 | tf_op jit(solution)/shard_map/ppermute | solution.py:188
  28.9 0.0 copy-done
  28.9 5.4 %collective-permute-start.7 = (bf16[512,512]{1,0:T(8,128)(2,1)S(1)}, bf16[512,512]{1,0:T(8,128)(2,1)S(1)}, u32[]{:S(2)}, u32[]{:S(2)}) collective-permute-start(bf16[512,512]{1,0:T(8,128)(2,1)S(1)} %bitcast.13), channel_id=1, source_target_pairs={{0,448},{1,449},{2,450},{3,451},{4,452},{5,453},{6,454},{7,455},{8... | collective-permute-start | bytes 1572872 | tf_op jit(solution)/shard_map/ppermute | solution.py:188
  34.3 1.9 %collective-permute-start.3 = (bf16[512,512]{1,0:T(8,128)(2,1)S(1)}, bf16[512,512]{1,0:T(8,128)(2,1)S(1)}, u32[]{:S(2)}, u32[]{:S(2)}) collective-permute-start(bf16[512,512]{1,0:T(8,128)(2,1)S(1)} %bitcast.14), channel_id=1, source_target_pairs={{0,64},{1,65},{2,66},{3,67},{4,68},{5,69},{6,70},{7,71},{8,72},{9,... | collective-permute-start | bytes 1572872 | tf_op jit(solution)/shard_map/ppermute | solution.py:188
  36.2 10.2 %collective-permute-done.7.refs_4_ = bf16[512,512]{1,0:T(8,128)(2,1)S(1)} collective-permute-done((bf16[512,512]{1,0:T(8,128)(2,1)S(1)}, bf16[512,512]{1,0:T(8,128)(2,1)S(1)}, u32[]{:S(2)}, u32[]{:S(2)}) %collective-permute-start.7) | collective-permute-done | bytes 524320 | tf_op jit(solution)/shard_map/ppermute | solution.py:188
  46.4 5.6 %collective-permute-start.8 = (bf16[512,512]{1,0:T(8,128)(2,1)S(1)}, bf16[512,512]{1,0:T(8,128)(2,1)S(1)}, u32[]{:S(2)}, u32[]{:S(2)}) collective-permute-start(bf16[512,512]{1,0:T(8,128)(2,1)S(1)} %collective-permute-done.7.refs_4_), channel_id=1, source_target_pairs={{0,448},{1,449},{2,450},{3,451},{4,452},{5,453},{6,454},{7,455},{8... | collective-permute-start | bytes 1572872 | tf_op jit(solution)/shard_map/ppermute | solution.py:188
  52.0 0.0 collective-permute-done.3.refs_9_
  52.1 1.9 %collective-permute-start.4 = (bf16[512,512]{1,0:T(8,128)(2,1)S(1)}, bf16[512,512]{1,0:T(8,128)(2,1)S(1)}, u32[]{:S(2)}, u32[]{:S(2)}) collective-permute-start(bf16[512,512]{1,0:T(8,128)(2,1)S(1)} %collective-permute-done.3.refs_9_), channel_id=1, source_target_pairs={{0,64},{1,65},{2,66},{3,67},{4,68},{5,69},{6,70},{7,71},{8,72},{9,... | collective-permute-start | bytes 1572872 | tf_op jit(solution)/shard_map/ppermute | solution.py:188
  54.0 0.0 collective-permute-done.1.refs_1_
  54.0 1.9 %collective-permute-start.11 = (bf16[2,2,512,256]{3,2,1,0:T(8,128)(2,1)S(1)}, bf16[2,2,512,256]{3,2,1,0:T(8,128)(2,1)S(1)}, u32[]{:S(2)}, u32[]{:S(2)}) collective-permute-start(bf16[2,2,512,256]{3,2,1,0:T(8,128)(2,1)S(1)} %collective-permute-done.1.refs_1_), channel_id=1, source_target_pairs={{0,4},{1,5},{2,6},{3,7},{4,0},{5,1},{6,2},{7,3},{8,12},{9,13},{10,... | collective-permute-start | bytes 3145736 | tf_op jit(solution)/shard_map/ppermute | solution.py:188
  55.9 1.9 %collective-permute-start.2 = (bf16[2,2,512,256]{3,2,1,0:T(8,128)(2,1)S(1)}, bf16[2,2,512,256]{3,2,1,0:T(8,128)(2,1)S(1)}, u32[]{:S(2)}, u32[]{:S(2)}) collective-permute-start(bf16[2,2,512,256]{3,2,1,0:T(8,128)(2,1)S(1)} %collective-permute-done.1.refs_1_), channel_id=1, source_target_pairs={{0,16},{1,17},{2,18},{3,19},{4,52},{5,53},{6,54},{7,55},{8,24},{9,... | collective-permute-start | bytes 3145736 | tf_op jit(solution)/shard_map/ppermute | solution.py:188
  57.9 5.6 %collective-permute-done.8.refs_5_ = bf16[512,512]{1,0:T(8,128)(2,1)S(1)} collective-permute-done((bf16[512,512]{1,0:T(8,128)(2,1)S(1)}, bf16[512,512]{1,0:T(8,128)(2,1)S(1)}, u32[]{:S(2)}, u32[]{:S(2)}) %collective-permute-start.8) | collective-permute-done | bytes 524320 | tf_op jit(solution)/shard_map/ppermute | solution.py:188
  63.5 5.6 %collective-permute-start.9 = (bf16[512,512]{1,0:T(8,128)(2,1)S(1)}, bf16[512,512]{1,0:T(8,128)(2,1)S(1)}, u32[]{:S(2)}, u32[]{:S(2)}) collective-permute-start(bf16[512,512]{1,0:T(8,128)(2,1)S(1)} %collective-permute-done.8.refs_5_), channel_id=1, source_target_pairs={{0,448},{1,449},{2,450},{3,451},{4,452},{5,453},{6,454},{7,455},{8... | collective-permute-start | bytes 1572872 | tf_op jit(solution)/shard_map/ppermute | solution.py:188
  69.1 0.0 collective-permute-done.4.refs_8_
  69.1 1.9 %collective-permute-start.5 = (bf16[512,512]{1,0:T(8,128)(2,1)S(1)}, bf16[512,512]{1,0:T(8,128)(2,1)S(1)}, u32[]{:S(2)}, u32[]{:S(2)}) collective-permute-start(bf16[512,512]{1,0:T(8,128)(2,1)S(1)} %collective-permute-done.4.refs_8_), channel_id=1, source_target_pairs={{0,64},{1,65},{2,66},{3,67},{4,68},{5,69},{6,70},{7,71},{8,72},{9,... | collective-permute-start | bytes 1572872 | tf_op jit(solution)/shard_map/ppermute | solution.py:188
  71.0 8.6 %collective-permute-done.9.refs_6_ = bf16[512,512]{1,0:T(8,128)(2,1)S(1)} collective-permute-done((bf16[512,512]{1,0:T(8,128)(2,1)S(1)}, bf16[512,512]{1,0:T(8,128)(2,1)S(1)}, u32[]{:S(2)}, u32[]{:S(2)}) %collective-permute-start.9) | collective-permute-done | bytes 524320 | tf_op jit(solution)/shard_map/ppermute | solution.py:188
  79.7 0.0 copy-start.2
  79.7 5.6 %collective-permute-start.10 = (bf16[256,512]{1,0:T(8,128)(2,1)S(1)}, bf16[256,512]{1,0:T(8,128)(2,1)S(1)}, u32[]{:S(2)}, u32[]{:S(2)}) collective-permute-start(bf16[256,512]{1,0:T(8,128)(2,1)S(1)} %slice.9), channel_id=1, source_target_pairs={{0,448},{1,449},{2,450},{3,451},{4,452},{5,453},{6,454},{7,455},{8... | collective-permute-start | bytes 786440 | tf_op jit(solution)/shard_map/ppermute | solution.py:188
  85.3 0.0 collective-permute-done.5.refs_7_
  85.3 0.0 copy-start.1
  85.3 1.9 %collective-permute-start.6 = (bf16[256,512]{1,0:T(8,128)(2,1)S(1)}, bf16[256,512]{1,0:T(8,128)(2,1)S(1)}, u32[]{:S(2)}, u32[]{:S(2)}) collective-permute-start(bf16[256,512]{1,0:T(8,128)(2,1)S(1)} %slice.8), channel_id=1, source_target_pairs={{0,64},{1,65},{2,66},{3,67},{4,68},{5,69},{6,70},{7,71},{8,72},{9,... | collective-permute-start | bytes 786440 | tf_op jit(solution)/shard_map/ppermute | solution.py:188
  87.3 0.0 collective-permute-done.11.refs_2_
  87.3 0.0 copy-done.2
  87.3 5.2 %early.1 = (f32[512,512]{1,0:T(8,128)S(1)}, bf16[2,512,512]{2,1,0:T(8,128)(2,1)S(1)}, bf16[512,512]{1,0:T(8,128)(2,1)S(1)}) custom-call(s32[6]{0:T(128)S(1)} %stack.36.at_ref, s32[64,64]{1,0:T(8,128)S(1)} %copy-done.2, bf16[2,2,512,256]{3,2,1,0:T(8,128)(2,1)S(1)} %pad_maximum_fusion.refs_0_, bf16[2,2,512,256]{3,2,1,0:T(8,128)(2,1)S(1)} %collective-permute-done.1.refs_1_, ...), custom_call_target="tpu_custom_call" | custom-call | flops 2147483648 | bytes 4194304 | tf_op jit(solution)/shard_map/early/pallas_call | solution.py:95
  92.5 0.0 collective-permute-done.10.s4b_ref
  92.6 2.3 %collective-permute-done.6.s4a_ref = bf16[256,512]{1,0:T(8,128)(2,1)S(1)} collective-permute-done((bf16[256,512]{1,0:T(8,128)(2,1)S(1)}, bf16[256,512]{1,0:T(8,128)(2,1)S(1)}, u32[]{:S(2)}, u32[]{:S(2)}) %collective-permute-start.6) | collective-permute-done | bytes 262176 | tf_op jit(solution)/shard_map/ppermute | solution.py:188
  94.8 0.0 collective-permute-done.2.x2_ref
  94.8 0.0 copy-done.1
  94.8 2.3 %shard_map.47 = f32[768,128]{1,0:T(8,128)S(1)} custom-call(s32[6]{0:T(128)S(1)} %stack.36.at_ref, s32[64,64]{1,0:T(8,128)S(1)} %copy-done.2, s32[64,64]{1,0:T(8,128)S(1)} %copy-done.1, bf16[2,2,512,256]{3,2,1,0:T(8,128)(2,1)S(1)} %collective-permute-done.2.x2_ref, bf16[256,512]{1,0:T(8,128)(2,1)S(1)} %collective-permute-done.6.s4a_ref, ...), custom_call_target="tpu_custom_call" | custom-call | flops 402653184 | bytes 1048576 | tf_op jit(solution)/shard_map/pallas_call | solution.py:148
  97.2 1.9 %collective-permute-start.12 = (f32[768,128]{1,0:T(8,128)S(1)}, f32[768,128]{1,0:T(8,128)S(1)}, u32[]{:S(2)}, u32[]{:S(2)}) collective-permute-start(f32[768,128]{1,0:T(8,128)S(1)} %shard_map.47), channel_id=1, source_target_pairs={{0,1},{1,0},{2,3},{3,2},{4,5},{5,4},{6,7},{7,6},{8,9},{9,8},{10,11... | collective-permute-start | bytes 1179656 | tf_op jit(solution)/shard_map/ppermute | solution.py:188
  99.1 2.4 %shard_map.46.own_ref = f32[768,128]{1,0:T(8,128)S(1)} custom-call(s32[6]{0:T(128)S(1)} %stack.36.at_ref, s32[64,64]{1,0:T(8,128)S(1)} %copy-done.2, s32[64,64]{1,0:T(8,128)S(1)} %copy-done.1, bf16[2,2,512,256]{3,2,1,0:T(8,128)(2,1)S(1)} %collective-permute-done.2.x2_ref, bf16[256,512]{1,0:T(8,128)(2,1)S(1)} %collective-permute-done.6.s4a_ref, ...), custom_call_target="tpu_custom_call" | custom-call | flops 402653184 | bytes 1048576 | tf_op jit(solution)/shard_map/pallas_call | solution.py:148
  101.5 5.6 %collective-permute-done.12.got_ref = f32[768,128]{1,0:T(8,128)S(1)} collective-permute-done((f32[768,128]{1,0:T(8,128)S(1)}, f32[768,128]{1,0:T(8,128)S(1)}, u32[]{:S(2)}, u32[]{:S(2)}) %collective-permute-start.12) | collective-permute-done | bytes 393248 | tf_op jit(solution)/shard_map/ppermute | solution.py:188
  107.1 1.8 %finish.1 = bf16[256,512]{1,0:T(8,128)(2,1)} custom-call(s32[6]{0:T(128)S(1)} %stack.36.at_ref, s32[64,64]{1,0:T(8,128)S(1)} %copy-done.1, f32[768,128]{1,0:T(8,128)S(1)} %shard_map.46.own_ref, f32[768,128]{1,0:T(8,128)S(1)} %collective-permute-done.12.got_ref), custom_call_target="tpu_custom_call" | custom-call | flops 1048576 | bytes 2097152 | tf_op jit(solution)/shard_map/finish/pallas_call | solution.py:168
  (3 shorter events, 0.1 us)
Async XLA Ops:
  0.0 28.9 %copy-start = (bf16[1024,512]{1,0:T(8,128)(2,1)S(1)}, bf16[1024,512]{1,0:T(8,128)(2,1)}, u32[]{:S(2)}) copy-start(bf16[1024,512]{1,0:T(8,128)(2,1)} %param.5) | copy-start | bytes 3145732
  1.2 21.9 %collective-permute-start = (bf16[512,256]{1,0:T(8,128)(2,1)S(1)}, bf16[512,256]{1,0:T(8,128)(2,1)S(1)}, u32[]{:S(2)}, u32[]{:S(2)}) collective-permute-start(bf16[512,256]{1,0:T(8,128)(2,1)S(1)} %get-tuple-element.18), channel_id=1, source_target_pairs={{0,10},{1,11},{2,8},{3,9},{4,14},{5,15},{6,12},{7,13},{8,2},{9,3},... | collective-permute-start | bytes 786440 | tf_op jit(solution)/shard_map/ppermute | solution.py:188
  25.4 28.6 %collective-permute-start.1 = (bf16[2,2,512,256]{3,2,1,0:T(8,128)(2,1)S(1)}, bf16[2,2,512,256]{3,2,1,0:T(8,128)(2,1)S(1)}, u32[]{:S(2)}, u32[]{:S(2)}) collective-permute-start(bf16[2,2,512,256]{3,2,1,0:T(8,128)(2,1)S(1)} %pad_maximum_fusion.refs_0_), channel_id=1, source_target_pairs={{0,16},{1,17},{2,18},{3,19},{4,52},{5,53},{6,54},{7,55},{8,24},{9,... | collective-permute-start | bytes 3145736 | tf_op jit(solution)/shard_map/ppermute | solution.py:188
  28.9 17.5 %collective-permute-start.7 = (bf16[512,512]{1,0:T(8,128)(2,1)S(1)}, bf16[512,512]{1,0:T(8,128)(2,1)S(1)}, u32[]{:S(2)}, u32[]{:S(2)}) collective-permute-start(bf16[512,512]{1,0:T(8,128)(2,1)S(1)} %bitcast.13), channel_id=1, source_target_pairs={{0,448},{1,449},{2,450},{3,451},{4,452},{5,453},{6,454},{7,455},{8... | collective-permute-start | bytes 1572872 | tf_op jit(solution)/shard_map/ppermute | solution.py:188
  34.3 17.8 %collective-permute-start.3 = (bf16[512,512]{1,0:T(8,128)(2,1)S(1)}, bf16[512,512]{1,0:T(8,128)(2,1)S(1)}, u32[]{:S(2)}, u32[]{:S(2)}) collective-permute-start(bf16[512,512]{1,0:T(8,128)(2,1)S(1)} %bitcast.14), channel_id=1, source_target_pairs={{0,64},{1,65},{2,66},{3,67},{4,68},{5,69},{6,70},{7,71},{8,72},{9,... | collective-permute-start | bytes 1572872 | tf_op jit(solution)/shard_map/ppermute | solution.py:188
  46.4 17.0 %collective-permute-start.8 = (bf16[512,512]{1,0:T(8,128)(2,1)S(1)}, bf16[512,512]{1,0:T(8,128)(2,1)S(1)}, u32[]{:S(2)}, u32[]{:S(2)}) collective-permute-start(bf16[512,512]{1,0:T(8,128)(2,1)S(1)} %collective-permute-done.7.refs_4_), channel_id=1, source_target_pairs={{0,448},{1,449},{2,450},{3,451},{4,452},{5,453},{6,454},{7,455},{8... | collective-permute-start | bytes 1572872 | tf_op jit(solution)/shard_map/ppermute | solution.py:188
  52.1 17.0 %collective-permute-start.4 = (bf16[512,512]{1,0:T(8,128)(2,1)S(1)}, bf16[512,512]{1,0:T(8,128)(2,1)S(1)}, u32[]{:S(2)}, u32[]{:S(2)}) collective-permute-start(bf16[512,512]{1,0:T(8,128)(2,1)S(1)} %collective-permute-done.3.refs_9_), channel_id=1, source_target_pairs={{0,64},{1,65},{2,66},{3,67},{4,68},{5,69},{6,70},{7,71},{8,72},{9,... | collective-permute-start | bytes 1572872 | tf_op jit(solution)/shard_map/ppermute | solution.py:188
  54.0 33.3 %collective-permute-start.11 = (bf16[2,2,512,256]{3,2,1,0:T(8,128)(2,1)S(1)}, bf16[2,2,512,256]{3,2,1,0:T(8,128)(2,1)S(1)}, u32[]{:S(2)}, u32[]{:S(2)}) collective-permute-start(bf16[2,2,512,256]{3,2,1,0:T(8,128)(2,1)S(1)} %collective-permute-done.1.refs_1_), channel_id=1, source_target_pairs={{0,4},{1,5},{2,6},{3,7},{4,0},{5,1},{6,2},{7,3},{8,12},{9,13},{10,... | collective-permute-start | bytes 3145736 | tf_op jit(solution)/shard_map/ppermute | solution.py:188
  55.9 38.9 %collective-permute-start.2 = (bf16[2,2,512,256]{3,2,1,0:T(8,128)(2,1)S(1)}, bf16[2,2,512,256]{3,2,1,0:T(8,128)(2,1)S(1)}, u32[]{:S(2)}, u32[]{:S(2)}) collective-permute-start(bf16[2,2,512,256]{3,2,1,0:T(8,128)(2,1)S(1)} %collective-permute-done.1.refs_1_), channel_id=1, source_target_pairs={{0,16},{1,17},{2,18},{3,19},{4,52},{5,53},{6,54},{7,55},{8,24},{9,... | collective-permute-start | bytes 3145736 | tf_op jit(solution)/shard_map/ppermute | solution.py:188
  63.5 16.2 %collective-permute-start.9 = (bf16[512,512]{1,0:T(8,128)(2,1)S(1)}, bf16[512,512]{1,0:T(8,128)(2,1)S(1)}, u32[]{:S(2)}, u32[]{:S(2)}) collective-permute-start(bf16[512,512]{1,0:T(8,128)(2,1)S(1)} %collective-permute-done.8.refs_5_), channel_id=1, source_target_pairs={{0,448},{1,449},{2,450},{3,451},{4,452},{5,453},{6,454},{7,455},{8... | collective-permute-start | bytes 1572872 | tf_op jit(solution)/shard_map/ppermute | solution.py:188
  69.1 16.2 %collective-permute-start.5 = (bf16[512,512]{1,0:T(8,128)(2,1)S(1)}, bf16[512,512]{1,0:T(8,128)(2,1)S(1)}, u32[]{:S(2)}, u32[]{:S(2)}) collective-permute-start(bf16[512,512]{1,0:T(8,128)(2,1)S(1)} %collective-permute-done.4.refs_8_), channel_id=1, source_target_pairs={{0,64},{1,65},{2,66},{3,67},{4,68},{5,69},{6,70},{7,71},{8,72},{9,... | collective-permute-start | bytes 1572872 | tf_op jit(solution)/shard_map/ppermute | solution.py:188
  79.7 7.6 %copy-start.2 = (s32[64,64]{1,0:T(8,128)S(1)}, s32[64,64]{1,0:T(8,128)}, u32[]{:S(2)}) copy-start(s32[64,64]{1,0:T(8,128)} %pattern_ref.5) | copy-start | bytes 49156
  79.7 12.9 %collective-permute-start.10 = (bf16[256,512]{1,0:T(8,128)(2,1)S(1)}, bf16[256,512]{1,0:T(8,128)(2,1)S(1)}, u32[]{:S(2)}, u32[]{:S(2)}) collective-permute-start(bf16[256,512]{1,0:T(8,128)(2,1)S(1)} %slice.9), channel_id=1, source_target_pairs={{0,448},{1,449},{2,450},{3,451},{4,452},{5,453},{6,454},{7,455},{8... | collective-permute-start | bytes 786440 | tf_op jit(solution)/shard_map/ppermute | solution.py:188
  85.3 9.5 %copy-start.1 = (s32[64,64]{1,0:T(8,128)S(1)}, s32[64,64]{1,0:T(8,128)}, u32[]{:S(2)}) copy-start(s32[64,64]{1,0:T(8,128)} %keep_ref.5) | copy-start | bytes 49156
  85.3 9.5 %collective-permute-start.6 = (bf16[256,512]{1,0:T(8,128)(2,1)S(1)}, bf16[256,512]{1,0:T(8,128)(2,1)S(1)}, u32[]{:S(2)}, u32[]{:S(2)}) collective-permute-start(bf16[256,512]{1,0:T(8,128)(2,1)S(1)} %slice.8), channel_id=1, source_target_pairs={{0,64},{1,65},{2,66},{3,67},{4,68},{5,69},{6,70},{7,71},{8,72},{9,... | collective-permute-start | bytes 786440 | tf_op jit(solution)/shard_map/ppermute | solution.py:188
  97.2 9.9 %collective-permute-start.12 = (f32[768,128]{1,0:T(8,128)S(1)}, f32[768,128]{1,0:T(8,128)S(1)}, u32[]{:S(2)}, u32[]{:S(2)}) collective-permute-start(f32[768,128]{1,0:T(8,128)S(1)} %shard_map.47), channel_id=1, source_target_pairs={{0,1},{1,0},{2,3},{3,2},{4,5},{5,4},{6,7},{7,6},{8,9},{9,8},{10,11... | collective-permute-start | bytes 1179656 | tf_op jit(solution)/shard_map/ppermute | solution.py:188

commit v2 on v1

v2 whole, which is shorter than its diff:
```python
import functools

import jax
import jax.numpy as jnp
from jax import lax
from jax.experimental import pallas as pl
from jax.experimental.pallas import tpu as pltpu
from jax.sharding import PartitionSpec as P


BLK = 128
AXES = ("row", "col", "layer")
ROWS, XS, LAYERS = 8, 4, 4
KEPT = 6


def table(move):
    pairs = []
    for r in range(ROWS):
        for x in range(XS):
            for z in range(2):
                for k in range(2):
                    for l in range(LAYERS):
                        r2, x2, z2, k2, l2 = move(r, x, z, k, l)
                        here = (r * 16 + x * 4 + z * 2 + k) * LAYERS + l
                        there = ((r2 % ROWS) * 16 + (x2 % XS) * 4 + z2 * 2 + k2) * LAYERS + l2
                        pairs.append((here, there))
    return pairs


ALONG_X = table(lambda r, x, z, k, l: (r, x + 1 - 2 * k, z, k, l))
ACROSS_Z = table(lambda r, x, z, k, l: (r, x, 1 - z, k, l ^ 2))
OTHER_CORE = table(lambda r, x, z, k, l: (r, x, z, 1 - k, l))
CORE_PAIRS = [[2 * i, 2 * i + 1] for i in range(8)]


def both_cores(value):
    return lax.all_gather(value, "col", axis=0, tiled=False, axis_index_groups=CORE_PAIRS)


SMEM = pl.BlockSpec(memory_space=pltpu.SMEM)
VMEM = pl.BlockSpec(memory_space=pltpu.VMEM)


def place(xs_ref, column, slab, row, lines, pattern_ref, at_ref):
    y, l = at_ref[0], at_ref[4]
    for g in range(2):
        for b in range(2):
            spot = pl.ds(pl.multiple_of(column + g * 2 * BLK + b * BLK, BLK), BLK)
            which = row * 8 + g * 4 + lax.rem(l, 2) * 2 + b
            for i in range(lines):
                part = slab[g, i * BLK:(i + 1) * BLK, b * BLK:(b + 1) * BLK]
                stored = pattern_ref[y * 8 + lax.div(l, 2) * 4 + i, which] == 1
                xs_ref[i * BLK:(i + 1) * BLK, spot] = jnp.where(stored, part, jnp.zeros_like(part))


def early_kernel(at_ref, pattern_ref, *refs):
    slabs, pieces, (out_ref, xs4_ref, xs_ref) = refs[:8], refs[8:15], refs[15:]
    y, x, z, k = (at_ref[i] for i in range(4))
    d = 1 - 2 * k
    places = [(x_at, zsel) for zsel in range(2) for x_at in (x, x - d, x + d, x + 2)]
    for slab, (x_at, zsel) in zip(slabs, places):
        row = 2 * lax.rem(x_at + 8, XS) + lax.rem(z + zsel, 2)
        step = lax.rem(row - y + 8, ROWS)
        column = jnp.where(step < 4, step, jnp.where(step == 4, 7, step - 1)) * 4 * BLK
        place(xs_ref, column, slab, row, 4, pattern_ref, at_ref)
    xs4_ref[...] = xs_ref[:, 28 * BLK:]
    for i in range(2):
        lines = slice(i * 2 * BLK, (i + 1) * 2 * BLK)
        right = jnp.concatenate([piece[...] for piece in pieces], axis=0)
        out_ref[lines, :] = jnp.dot(xs_ref[lines, :28 * BLK], right, preferred_element_type=jnp.float32)


def early(at, pattern, slabs, pieces):
    return pl.pallas_call(
        early_kernel,
        out_shape=(
            jax.ShapeDtypeStruct((512, 512), jnp.float32),
            jax.ShapeDtypeStruct((512, 512), jnp.bfloat16),
        ),
        in_specs=[SMEM] * 2 + [VMEM] * 15,
        out_specs=(VMEM,) * 2,
        scratch_shapes=[pltpu.VMEM((512, 4096), jnp.bfloat16)],
        compiler_params=pltpu.CompilerParams(vmem_limit_bytes=16 * 2**20),
        cost_estimate=pl.CostEstimate(flops=2 * 512 * 3584 * 512, bytes_accessed=4 * 2**20, transcendentals=0),
        name="early",
    )(at, pattern, *slabs, *pieces)


def kept(keep_ref, at_ref, region):
    y, c = at_ref[0], at_ref[5]
    flags = [keep_ref[y * 8 + region * 2 + a, c * 4 + b] == 1 for a in range(2) for b in range(4)]
    spots, at = [], jnp.int32(0)
    for flag in flags:
        spots.append(pl.ds(pl.multiple_of(jnp.minimum(at, KEPT - 1) * BLK, BLK), BLK))
        at = at + flag.astype(jnp.int32)
    return flags, spots


def late_kernel(shift, at_ref, keep_ref, s4_ref, xs4_ref, sum_ref, out_ref):
    l = at_ref[4]
    part = lax.rem(l + shift, 2)
    lines = pl.ds(pl.multiple_of(part * 2 * BLK, 2 * BLK), 2 * BLK)
    value = sum_ref[lines, :] + jnp.dot(xs4_ref[lines, :], s4_ref[...], preferred_element_type=jnp.float32)
    flags, spots = kept(keep_ref, at_ref, lax.div(l, 2) * 2 + part)
    for i, (flag, spot) in enumerate(zip(flags, spots)):
        a, b = i // 4, i % 4

        @pl.when(flag)
        def _():
            out_ref[spot, :] = value[a * BLK:(a + 1) * BLK, b * BLK:(b + 1) * BLK]


def late(shift, at, keep, *arrays):
    return pl.pallas_call(
        functools.partial(late_kernel, shift),
        out_shape=jax.ShapeDtypeStruct((KEPT * BLK, BLK), jnp.float32),
        in_specs=[SMEM] * 2 + [VMEM] * 3,
        out_specs=VMEM,
        compiler_params=pltpu.CompilerParams(vmem_limit_bytes=8 * 2**20),
        cost_estimate=pl.CostEstimate(flops=2 * 256 * 512 * 512, bytes_accessed=2**20, transcendentals=0),
    )(at, keep, *arrays)


def finish_kernel(at_ref, keep_ref, own_ref, got_ref, out_ref):
    flags, spots = kept(keep_ref, at_ref, at_ref[4])
    for i, (flag, spot) in enumerate(zip(flags, spots)):
        a, b = i // 4, i % 4
        total = jnp.where(flag, own_ref[spot, :] + got_ref[spot, :], 0.0)
        out_ref[a * BLK:(a + 1) * BLK, b * BLK:(b + 1) * BLK] = total.astype(jnp.bfloat16)


def finish(at, keep, own, got):
    return pl.pallas_call(
        finish_kernel,
        out_shape=jax.ShapeDtypeStruct((2 * BLK, 4 * BLK), jnp.bfloat16),
        in_specs=[SMEM, SMEM, VMEM, VMEM],
        out_specs=VMEM,
        compiler_params=pltpu.CompilerParams(vmem_limit_bytes=8 * 2**20),
        cost_estimate=pl.CostEstimate(flops=2**20, bytes_accessed=2 * 2**20, transcendentals=0),
        name="finish",
    )(at, keep, own, got)


def body(sign_iterate, square, pattern, keep):
    l = lax.axis_index("layer")
    y = lax.axis_index("row")
    c = lax.axis_index("col")
    half, part = l // 2, l % 2
    at = jnp.stack([y, c // 4, (c // 2) % 2, c % 2, l, c]).astype(jnp.int32)
    at, sign_iterate, square = lax.optimization_barrier((at, sign_iterate, square))

    def step(value, pairs):
        return lax.ppermute(value, AXES, pairs)

    def down(value, shift):
        return step(value, table(lambda r, x, z, k, l: (r + shift, x, z, k, l)))

    def slab(rows):
        return lax.dynamic_slice(sign_iterate, (rows * 512, part * 256), (512, 256))

    s0 = lax.dynamic_index_in_dim(square.reshape(2, 2, 256, 512), part, 1, False).reshape(512, 512)
    s7 = down(s0, 1)
    z_own = step(slab(1 - half), ACROSS_Z)
    s1 = down(s0, -1)
    x0 = both_cores(slab(half))
    x1 = step(x0, ALONG_X)
    s6 = down(s7, 1)
    z0 = both_cores(z_own)
    z1 = step(z0, ALONG_X)
    s2 = down(s1, -1)
    s5 = down(s6, 1)
    x2 = step(x1, ALONG_X)
    z2 = step(z1, ALONG_X)
    s3 = down(s2, -1)
    s4 = down(s5, 1)
    x1o = step(x1, OTHER_CORE)
    z1o = step(z1, OTHER_CORE)
    total, xs4 = early(at, pattern, (x0, x1, x1o, x2, z0, z1, z1o, z2), (s0, s1, s2, s3, s5, s6, s7))
    sent = late(1, at, keep, s4, xs4, total)
    got = step(sent, table(lambda r, x, z, k, l: (r, x, z, k, l ^ 1)))
    own = late(0, at, keep, s4, xs4, total)
    return finish(at, keep, own, got)


def solution(mesh):
    return jax.shard_map(
        body,
        mesh=mesh,
        in_specs=(P("row", "col"), P("row", "col"), P(), P()),
        out_specs=P(("row", "layer"), "col"),
        check_vma=False,
    )
```

time: 109 us -> 98.7 us (0.906)
  the two profiles are of different devices: /device:TPU:64 before, /device:TPU:30 now
where the time goes in v2:
time: 98.7 us; the launch traced here: 98.1 us
  starting transfers between devices  57 us (58%)
  waiting for transfers between devices  25.9 us (26%)
  Pallas kernels  9.27 us (9%)
  blocking collectives  4.35 us (4%)
  local copies, waits for them, and re-layouts  1.31 us (1%)
    ppermute x15, starting transfers between devices, step(): return lax.ppermute(value, AXES, pairs)  57 us
    ppermute x15, waiting for transfers between devices, step(): return lax.ppermute(value, AXES, pairs)  25.9 us
    pallas_call x1, Pallas kernels, early(): pl.pallas_call(early_kernel, out_shape=(jax.ShapeDtypeStruct((512, 512),...  4.58 us
    all_gather x2, blocking collectives, both_cores(): lax.all_gather(value, 'col', axis=0, tiled=False, axis_index_groups=CORE_...  4.35 us
    pallas_call x2, Pallas kernels, late(): pl.pallas_call(functools.partial(late_kernel, shift), out_shape=jax.Shape...  2.84 us
  transfers between devices with their start and end apart: 15, of which 4 were waited for; matrix products, arithmetic and copies ran while one was open for 0% of the time, Pallas kernels for 6%

profile of v2, /device:TPU:30, one launch (start us, length us, event | category | flops | bytes accessed | tf_op | source)
XLA Modules:
  0.0 98.1 jit_solution(3115852099707983783)
XLA Ops:
  0.0 0.0 copy-start
  0.0 0.0 copy-start.3
  0.0 0.1 stack.27.at_ref
  0.1 1.1 %copy-done = bf16[1024,512]{1,0:T(8,128)(2,1)S(1)} copy-done((bf16[1024,512]{1,0:T(8,128)(2,1)S(1)}, bf16[1024,512]{1,0:T(8,128)(2,1)}, u32[]{:S(2)}) %copy-start) | copy-done | bytes 1048600
  1.3 4.7 %collective-permute-start = (bf16[512,512]{1,0:T(8,128)(2,1)S(1)}, bf16[512,512]{1,0:T(8,128)(2,1)S(1)}, u32[]{:S(2)}, u32[]{:S(2)}) collective-permute-start(bf16[512,512]{1,0:T(8,128)(2,1)S(1)} %bitcast.17), channel_id=1, source_target_pairs={{0,64},{1,65},{2,66},{3,67},{4,68},{5,69},{6,70},{7,71},{8,72},{9,... | collective-permute-start | bytes 1572872 | tf_op jit(solution)/shard_map/ppermute | solution.py:154
  6.0 0.0 copy-done.3
  6.1 2.2 %all-gather = bf16[1024,256]{1,0:T(8,128)(2,1)S(1)} all-gather(bf16[512,256]{1,0:T(8,128)(2,1)S(1)} %get-tuple-element.16), channel_id=2, replica_groups={{0,4},{8,12},{16,20},{24,28},{32,36},{40,44},{48,52},{56,60},{1,5},{9,1..., dimensions={0}, use_global_device_ids=true | all-gather | bytes 786432 | tf_op jit(solution)/shard_map/all_gather | solution.py:38
  8.2 2.4 %collective-permute-start.4 = (bf16[2,512,256]{2,1,0:T(8,128)(2,1)S(1)}, bf16[2,512,256]{2,1,0:T(8,128)(2,1)S(1)}, u32[]{:S(2)}, u32[]{:S(2)}) collective-permute-start(bf16[2,512,256]{2,1,0:T(8,128)(2,1)S(1)} %bitcast.13), channel_id=1, source_target_pairs={{0,16},{1,17},{2,18},{3,19},{4,52},{5,53},{6,54},{7,55},{8,24},{9,... | collective-permute-start | bytes 1572872 | tf_op jit(solution)/shard_map/ppermute | solution.py:154
  10.6 1.9 %collective-permute-start.11 = (bf16[512,512]{1,0:T(8,128)(2,1)S(1)}, bf16[512,512]{1,0:T(8,128)(2,1)S(1)}, u32[]{:S(2)}, u32[]{:S(2)}) collective-permute-start(bf16[512,512]{1,0:T(8,128)(2,1)S(1)} %bitcast.18), channel_id=1, source_target_pairs={{0,448},{1,449},{2,450},{3,451},{4,452},{5,453},{6,454},{7,455},{8... | collective-permute-start | bytes 1572872 | tf_op jit(solution)/shard_map/ppermute | solution.py:154
  12.6 0.0 copy-start.2
  12.6 10.9 %collective-permute-start.7 = (bf16[512,256]{1,0:T(8,128)(2,1)S(1)}, bf16[512,256]{1,0:T(8,128)(2,1)S(1)}, u32[]{:S(2)}, u32[]{:S(2)}) collective-permute-start(bf16[512,256]{1,0:T(8,128)(2,1)S(1)} %get-tuple-element.15), channel_id=1, source_target_pairs={{0,10},{1,11},{2,8},{3,9},{4,14},{5,15},{6,12},{7,13},{8,2},{9,3},... | collective-permute-start | bytes 786440 | tf_op jit(solution)/shard_map/ppermute | solution.py:154
  23.5 0.0 collective-permute-done.refs_14_
  23.5 5.1 %collective-permute-start.1 = (bf16[512,512]{1,0:T(8,128)(2,1)S(1)}, bf16[512,512]{1,0:T(8,128)(2,1)S(1)}, u32[]{:S(2)}, u32[]{:S(2)}) collective-permute-start(bf16[512,512]{1,0:T(8,128)(2,1)S(1)} %collective-permute-done.refs_14_), channel_id=1, source_target_pairs={{0,64},{1,65},{2,66},{3,67},{4,68},{5,69},{6,70},{7,71},{8,72},{9,... | collective-permute-start | bytes 1572872 | tf_op jit(solution)/shard_map/ppermute | solution.py:154
  28.7 6.4 %collective-permute-done.7 = bf16[512,256]{1,0:T(8,128)(2,1)S(1)} collective-permute-done((bf16[512,256]{1,0:T(8,128)(2,1)S(1)}, bf16[512,256]{1,0:T(8,128)(2,1)S(1)}, u32[]{:S(2)}, u32[]{:S(2)}) %collective-permute-start.7) | collective-permute-done | bytes 262176 | tf_op jit(solution)/shard_map/ppermute | solution.py:154
  35.0 2.2 %all-gather.1 = bf16[1024,256]{1,0:T(8,128)(2,1)S(1)} all-gather(bf16[512,256]{1,0:T(8,128)(2,1)S(1)} %collective-permute-done.7), channel_id=3, replica_groups={{0,4},{8,12},{16,20},{24,28},{32,36},{40,44},{48,52},{56,60},{1,5},{9,1..., dimensions={0}, use_global_device_ids=true | all-gather | bytes 786432 | tf_op jit(solution)/shard_map/all_gather | solution.py:38
  37.2 0.0 copy-start.1
  37.2 4.1 %collective-permute-start.8 = (bf16[2,512,256]{2,1,0:T(8,128)(2,1)S(1)}, bf16[2,512,256]{2,1,0:T(8,128)(2,1)S(1)}, u32[]{:S(2)}, u32[]{:S(2)}) collective-permute-start(bf16[2,512,256]{2,1,0:T(8,128)(2,1)S(1)} %bitcast.15), channel_id=1, source_target_pairs={{0,16},{1,17},{2,18},{3,19},{4,52},{5,53},{6,54},{7,55},{8,24},{9,... | collective-permute-start | bytes 1572872 | tf_op jit(solution)/shard_map/ppermute | solution.py:154
  41.3 0.0 collective-permute-done.4.refs_1_
  41.4 1.9 %collective-permute-start.5 = (bf16[2,512,256]{2,1,0:T(8,128)(2,1)S(1)}, bf16[2,512,256]{2,1,0:T(8,128)(2,1)S(1)}, u32[]{:S(2)}, u32[]{:S(2)}) collective-permute-start(bf16[2,512,256]{2,1,0:T(8,128)(2,1)S(1)} %collective-permute-done.4.refs_1_), channel_id=1, source_target_pairs={{0,4},{1,5},{2,6},{3,7},{4,0},{5,1},{6,2},{7,3},{8,12},{9,13},{10,... | collective-permute-start | bytes 1572872 | tf_op jit(solution)/shard_map/ppermute | solution.py:154
  43.3 0.0 collective-permute-done.11.refs_9_
  43.3 1.9 %collective-permute-start.12 = (bf16[512,512]{1,0:T(8,128)(2,1)S(1)}, bf16[512,512]{1,0:T(8,128)(2,1)S(1)}, u32[]{:S(2)}, u32[]{:S(2)}) collective-permute-start(bf16[512,512]{1,0:T(8,128)(2,1)S(1)} %collective-permute-done.11.refs_9_), channel_id=1, source_target_pairs={{0,448},{1,449},{2,450},{3,451},{4,452},{5,453},{6,454},{7,455},{8... | collective-permute-start | bytes 1572872 | tf_op jit(solution)/shard_map/ppermute | solution.py:154
  45.2 0.0 collective-permute-done.1.refs_13_
  45.2 5.2 %collective-permute-start.2 = (bf16[512,512]{1,0:T(8,128)(2,1)S(1)}, bf16[512,512]{1,0:T(8,128)(2,1)S(1)}, u32[]{:S(2)}, u32[]{:S(2)}) collective-permute-start(bf16[512,512]{1,0:T(8,128)(2,1)S(1)} %collective-permute-done.1.refs_13_), channel_id=1, source_target_pairs={{0,64},{1,65},{2,66},{3,67},{4,68},{5,69},{6,70},{7,71},{8,72},{9,... | collective-permute-start | bytes 1572872 | tf_op jit(solution)/shard_map/ppermute | solution.py:154
  50.4 2.9 %collective-permute-start.6 = (bf16[2,512,256]{2,1,0:T(8,128)(2,1)S(1)}, bf16[2,512,256]{2,1,0:T(8,128)(2,1)S(1)}, u32[]{:S(2)}, u32[]{:S(2)}) collective-permute-start(bf16[2,512,256]{2,1,0:T(8,128)(2,1)S(1)} %collective-permute-done.4.refs_1_), channel_id=1, source_target_pairs={{0,16},{1,17},{2,18},{3,19},{4,52},{5,53},{6,54},{7,55},{8,24},{9,... | collective-permute-start | bytes 1572872 | tf_op jit(solution)/shard_map/ppermute | solution.py:154
  53.3 0.0 collective-permute-done.8.refs_5_
  53.3 3.0 %collective-permute-start.10 = (bf16[2,512,256]{2,1,0:T(8,128)(2,1)S(1)}, bf16[2,512,256]{2,1,0:T(8,128)(2,1)S(1)}, u32[]{:S(2)}, u32[]{:S(2)}) collective-permute-start(bf16[2,512,256]{2,1,0:T(8,128)(2,1)S(1)} %collective-permute-done.8.refs_5_), channel_id=1, source_target_pairs={{0,16},{1,17},{2,18},{3,19},{4,52},{5,53},{6,54},{7,55},{8,24},{9,... | collective-permute-start | bytes 1572872 | tf_op jit(solution)/shard_map/ppermute | solution.py:154
  56.3 0.0 collective-permute-done.5.refs_2_
  56.3 1.9 %collective-permute-start.9 = (bf16[2,512,256]{2,1,0:T(8,128)(2,1)S(1)}, bf16[2,512,256]{2,1,0:T(8,128)(2,1)S(1)}, u32[]{:S(2)}, u32[]{:S(2)}) collective-permute-start(bf16[2,512,256]{2,1,0:T(8,128)(2,1)S(1)} %collective-permute-done.8.refs_5_), channel_id=1, source_target_pairs={{0,4},{1,5},{2,6},{3,7},{4,0},{5,1},{6,2},{7,3},{8,12},{9,13},{10,... | collective-permute-start | bytes 1572872 | tf_op jit(solution)/shard_map/ppermute | solution.py:154
  58.2 2.8 %collective-permute-done.12.refs_10_ = bf16[512,512]{1,0:T(8,128)(2,1)S(1)} collective-permute-done((bf16[512,512]{1,0:T(8,128)(2,1)S(1)}, bf16[512,512]{1,0:T(8,128)(2,1)S(1)}, u32[]{:S(2)}, u32[]{:S(2)}) %collective-permute-start.12) | collective-permute-done | bytes 524320 | tf_op jit(solution)/shard_map/ppermute | solution.py:154
  61.0 1.9 %collective-permute-start.13 = (bf16[512,512]{1,0:T(8,128)(2,1)S(1)}, bf16[512,512]{1,0:T(8,128)(2,1)S(1)}, u32[]{:S(2)}, u32[]{:S(2)}) collective-permute-start(bf16[512,512]{1,0:T(8,128)(2,1)S(1)} %collective-permute-done.12.refs_10_), channel_id=1, source_target_pairs={{0,448},{1,449},{2,450},{3,451},{4,452},{5,453},{6,454},{7,455},{8... | collective-permute-start | bytes 1572872 | tf_op jit(solution)/shard_map/ppermute | solution.py:154
  63.0 0.0 collective-permute-done.2.refs_12_
  63.0 5.1 %collective-permute-start.3 = (bf16[512,512]{1,0:T(8,128)(2,1)S(1)}, bf16[512,512]{1,0:T(8,128)(2,1)S(1)}, u32[]{:S(2)}, u32[]{:S(2)}) collective-permute-start(bf16[512,512]{1,0:T(8,128)(2,1)S(1)} %collective-permute-done.2.refs_12_), channel_id=1, source_target_pairs={{0,64},{1,65},{2,66},{3,67},{4,68},{5,69},{6,70},{7,71},{8,72},{9,... | collective-permute-start | bytes 1572872 | tf_op jit(solution)/shard_map/ppermute | solution.py:154
  68.1 0.0 collective-permute-done.6.refs_3_
  68.1 0.0 collective-permute-done.10.refs_7_
  68.1 0.0 collective-permute-done.9.refs_6_
  68.1 9.7 %collective-permute-done.13.refs_11_ = bf16[512,512]{1,0:T(8,128)(2,1)S(1)} collective-permute-done((bf16[512,512]{1,0:T(8,128)(2,1)S(1)}, bf16[512,512]{1,0:T(8,128)(2,1)S(1)}, u32[]{:S(2)}, u32[]{:S(2)}) %collective-permute-start.13) | collective-permute-done | bytes 524320 | tf_op jit(solution)/shard_map/ppermute | solution.py:154
  77.9 0.0 copy-done.2
  77.9 4.6 %early.1 = (f32[512,512]{1,0:T(8,128)S(1)}, bf16[512,512]{1,0:T(8,128)(2,1)S(1)}) custom-call(s32[6]{0:T(128)S(1)} %stack.27.at_ref, s32[64,64]{1,0:T(8,128)S(1)} %copy-done.2, bf16[2,512,256]{2,1,0:T(8,128)(2,1)S(1)} %bitcast.14, bf16[2,512,256]{2,1,0:T(8,128)(2,1)S(1)} %collective-permute-done.4.refs_1_, ...), custom_call_target="tpu_custom_call" | custom-call | flops 1879048192 | bytes 4194304 | tf_op jit(solution)/shard_map/early/pallas_call | solution.py:75
  82.5 0.0 collective-permute-done.3.s4_ref
  82.5 0.0 copy-done.1
  82.5 1.4 %shard_map.47 = f32[768,128]{1,0:T(8,128)S(1)} custom-call(s32[6]{0:T(128)S(1)} %stack.27.at_ref, s32[64,64]{1,0:T(8,128)S(1)} %copy-done.1, bf16[512,512]{1,0:T(8,128)(2,1)S(1)} %collective-permute-done.3.s4_ref, bf16[512,512]{1,0:T(8,128)(2,1)S(1)} %get-tuple-element.13.xs4_ref, f32[512,512]{1,0:T(8,128)S(1)} %get-tuple-element.14.sum_ref), custom_call_target="tpu_custom_call" | custom-call | flops 134217728 | bytes 1048576 | tf_op jit(solution)/shard_map/pallas_call | solution.py:115
  83.9 4.0 %collective-permute-start.14 = (f32[768,128]{1,0:T(8,128)S(1)}, f32[768,128]{1,0:T(8,128)S(1)}, u32[]{:S(2)}, u32[]{:S(2)}) collective-permute-start(f32[768,128]{1,0:T(8,128)S(1)} %shard_map.47), channel_id=1, source_target_pairs={{0,1},{1,0},{2,3},{3,2},{4,5},{5,4},{6,7},{7,6},{8,9},{9,8},{10,11... | collective-permute-start | bytes 1179656 | tf_op jit(solution)/shard_map/ppermute | solution.py:154
  87.9 1.4 %shard_map.46.own_ref = f32[768,128]{1,0:T(8,128)S(1)} custom-call(s32[6]{0:T(128)S(1)} %stack.27.at_ref, s32[64,64]{1,0:T(8,128)S(1)} %copy-done.1, bf16[512,512]{1,0:T(8,128)(2,1)S(1)} %collective-permute-done.3.s4_ref, bf16[512,512]{1,0:T(8,128)(2,1)S(1)} %get-tuple-element.13.xs4_ref, f32[512,512]{1,0:T(8,128)S(1)} %get-tuple-element.14.sum_ref), custom_call_target="tpu_custom_call" | custom-call | flops 134217728 | bytes 1048576 | tf_op jit(solution)/shard_map/pallas_call | solution.py:115
  89.3 6.9 %collective-permute-done.14.got_ref = f32[768,128]{1,0:T(8,128)S(1)} collective-permute-done((f32[768,128]{1,0:T(8,128)S(1)}, f32[768,128]{1,0:T(8,128)S(1)}, u32[]{:S(2)}, u32[]{:S(2)}) %collective-permute-start.14) | collective-permute-done | bytes 393248 | tf_op jit(solution)/shard_map/ppermute | solution.py:154
  96.2 1.8 %finish.1 = bf16[256,512]{1,0:T(8,128)(2,1)} custom-call(s32[6]{0:T(128)S(1)} %stack.27.at_ref, s32[64,64]{1,0:T(8,128)S(1)} %copy-done.1, f32[768,128]{1,0:T(8,128)S(1)} %shard_map.46.own_ref, f32[768,128]{1,0:T(8,128)S(1)} %collective-permute-done.14.got_ref), custom_call_target="tpu_custom_call" | custom-call | flops 1048576 | bytes 2097152 | tf_op jit(solution)/shard_map/finish/pallas_call | solution.py:134
  (2 shorter events, 0.1 us)
Async XLA Ops:
  0.0 1.2 %copy-start = (bf16[1024,512]{1,0:T(8,128)(2,1)S(1)}, bf16[1024,512]{1,0:T(8,128)(2,1)}, u32[]{:S(2)}) copy-start(bf16[1024,512]{1,0:T(8,128)(2,1)} %param.5) | copy-start | bytes 3145732
  0.0 6.0 %copy-start.3 = (bf16[1024,512]{1,0:T(8,128)(2,1)S(1)}, bf16[1024,512]{1,0:T(8,128)(2,1)}, u32[]{:S(2)}) copy-start(bf16[1024,512]{1,0:T(8,128)(2,1)} %param.4) | copy-start | bytes 3145732
  1.3 22.2 %collective-permute-start = (bf16[512,512]{1,0:T(8,128)(2,1)S(1)}, bf16[512,512]{1,0:T(8,128)(2,1)S(1)}, u32[]{:S(2)}, u32[]{:S(2)}) collective-permute-start(bf16[512,512]{1,0:T(8,128)(2,1)S(1)} %bitcast.17), channel_id=1, source_target_pairs={{0,64},{1,65},{2,66},{3,67},{4,68},{5,69},{6,70},{7,71},{8,72},{9,... | collective-permute-start | bytes 1572872 | tf_op jit(solution)/shard_map/ppermute | solution.py:154
  8.2 33.1 %collective-permute-start.4 = (bf16[2,512,256]{2,1,0:T(8,128)(2,1)S(1)}, bf16[2,512,256]{2,1,0:T(8,128)(2,1)S(1)}, u32[]{:S(2)}, u32[]{:S(2)}) collective-permute-start(bf16[2,512,256]{2,1,0:T(8,128)(2,1)S(1)} %bitcast.13), channel_id=1, source_target_pairs={{0,16},{1,17},{2,18},{3,19},{4,52},{5,53},{6,54},{7,55},{8,24},{9,... | collective-permute-start | bytes 1572872 | tf_op jit(solution)/shard_map/ppermute | solution.py:154
  10.6 32.7 %collective-permute-start.11 = (bf16[512,512]{1,0:T(8,128)(2,1)S(1)}, bf16[512,512]{1,0:T(8,128)(2,1)S(1)}, u32[]{:S(2)}, u32[]{:S(2)}) collective-permute-start(bf16[512,512]{1,0:T(8,128)(2,1)S(1)} %bitcast.18), channel_id=1, source_target_pairs={{0,448},{1,449},{2,450},{3,451},{4,452},{5,453},{6,454},{7,455},{8... | collective-permute-start | bytes 1572872 | tf_op jit(solution)/shard_map/ppermute | solution.py:154
  12.6 65.3 %copy-start.2 = (s32[64,64]{1,0:T(8,128)S(1)}, s32[64,64]{1,0:T(8,128)}, u32[]{:S(2)}) copy-start(s32[64,64]{1,0:T(8,128)} %pattern_ref.1) | copy-start | bytes 49156
  12.6 22.5 %collective-permute-start.7 = (bf16[512,256]{1,0:T(8,128)(2,1)S(1)}, bf16[512,256]{1,0:T(8,128)(2,1)S(1)}, u32[]{:S(2)}, u32[]{:S(2)}) collective-permute-start(bf16[512,256]{1,0:T(8,128)(2,1)S(1)} %get-tuple-element.15), channel_id=1, source_target_pairs={{0,10},{1,11},{2,8},{3,9},{4,14},{5,15},{6,12},{7,13},{8,2},{9,3},... | collective-permute-start | bytes 786440 | tf_op jit(solution)/shard_map/ppermute | solution.py:154
  23.5 21.7 %collective-permute-start.1 = (bf16[512,512]{1,0:T(8,128)(2,1)S(1)}, bf16[512,512]{1,0:T(8,128)(2,1)S(1)}, u32[]{:S(2)}, u32[]{:S(2)}) collective-permute-start(bf16[512,512]{1,0:T(8,128)(2,1)S(1)} %collective-permute-done.refs_14_), channel_id=1, source_target_pairs={{0,64},{1,65},{2,66},{3,67},{4,68},{5,69},{6,70},{7,71},{8,72},{9,... | collective-permute-start | bytes 1572872 | tf_op jit(solution)/shard_map/ppermute | solution.py:154
  37.2 45.3 %copy-start.1 = (s32[64,64]{1,0:T(8,128)S(1)}, s32[64,64]{1,0:T(8,128)}, u32[]{:S(2)}) copy-start(s32[64,64]{1,0:T(8,128)} %keep_ref.5) | copy-start | bytes 49156
  37.2 16.1 %collective-permute-start.8 = (bf16[2,512,256]{2,1,0:T(8,128)(2,1)S(1)}, bf16[2,512,256]{2,1,0:T(8,128)(2,1)S(1)}, u32[]{:S(2)}, u32[]{:S(2)}) collective-permute-start(bf16[2,512,256]{2,1,0:T(8,128)(2,1)S(1)} %bitcast.15), channel_id=1, source_target_pairs={{0,16},{1,17},{2,18},{3,19},{4,52},{5,53},{6,54},{7,55},{8,24},{9,... | collective-permute-start | bytes 1572872 | tf_op jit(solution)/shard_map/ppermute | solution.py:154
  41.4 14.9 %collective-permute-start.5 = (bf16[2,512,256]{2,1,0:T(8,128)(2,1)S(1)}, bf16[2,512,256]{2,1,0:T(8,128)(2,1)S(1)}, u32[]{:S(2)}, u32[]{:S(2)}) collective-permute-start(bf16[2,512,256]{2,1,0:T(8,128)(2,1)S(1)} %collective-permute-done.4.refs_1_), channel_id=1, source_target_pairs={{0,4},{1,5},{2,6},{3,7},{4,0},{5,1},{6,2},{7,3},{8,12},{9,13},{10,... | collective-permute-start | bytes 1572872 | tf_op jit(solution)/shard_map/ppermute | solution.py:154
  43.3 17.7 %collective-permute-start.12 = (bf16[512,512]{1,0:T(8,128)(2,1)S(1)}, bf16[512,512]{1,0:T(8,128)(2,1)S(1)}, u32[]{:S(2)}, u32[]{:S(2)}) collective-permute-start(bf16[512,512]{1,0:T(8,128)(2,1)S(1)} %collective-permute-done.11.refs_9_), channel_id=1, source_target_pairs={{0,448},{1,449},{2,450},{3,451},{4,452},{5,453},{6,454},{7,455},{8... | collective-permute-start | bytes 1572872 | tf_op jit(solution)/shard_map/ppermute | solution.py:154
  45.2 17.7 %collective-permute-start.2 = (bf16[512,512]{1,0:T(8,128)(2,1)S(1)}, bf16[512,512]{1,0:T(8,128)(2,1)S(1)}, u32[]{:S(2)}, u32[]{:S(2)}) collective-permute-start(bf16[512,512]{1,0:T(8,128)(2,1)S(1)} %collective-permute-done.1.refs_13_), channel_id=1, source_target_pairs={{0,64},{1,65},{2,66},{3,67},{4,68},{5,69},{6,70},{7,71},{8,72},{9,... | collective-permute-start | bytes 1572872 | tf_op jit(solution)/shard_map/ppermute | solution.py:154
  50.4 17.7 %collective-permute-start.6 = (bf16[2,512,256]{2,1,0:T(8,128)(2,1)S(1)}, bf16[2,512,256]{2,1,0:T(8,128)(2,1)S(1)}, u32[]{:S(2)}, u32[]{:S(2)}) collective-permute-start(bf16[2,512,256]{2,1,0:T(8,128)(2,1)S(1)} %collective-permute-done.4.refs_1_), channel_id=1, source_target_pairs={{0,16},{1,17},{2,18},{3,19},{4,52},{5,53},{6,54},{7,55},{8,24},{9,... | collective-permute-start | bytes 1572872 | tf_op jit(solution)/shard_map/ppermute | solution.py:154
  53.3 14.8 %collective-permute-start.10 = (bf16[2,512,256]{2,1,0:T(8,128)(2,1)S(1)}, bf16[2,512,256]{2,1,0:T(8,128)(2,1)S(1)}, u32[]{:S(2)}, u32[]{:S(2)}) collective-permute-start(bf16[2,512,256]{2,1,0:T(8,128)(2,1)S(1)} %collective-permute-done.8.refs_5_), channel_id=1, source_target_pairs={{0,16},{1,17},{2,18},{3,19},{4,52},{5,53},{6,54},{7,55},{8,24},{9,... | collective-permute-start | bytes 1572872 | tf_op jit(solution)/shard_map/ppermute | solution.py:154
  56.3 11.8 %collective-permute-start.9 = (bf16[2,512,256]{2,1,0:T(8,128)(2,1)S(1)}, bf16[2,512,256]{2,1,0:T(8,128)(2,1)S(1)}, u32[]{:S(2)}, u32[]{:S(2)}) collective-permute-start(bf16[2,512,256]{2,1,0:T(8,128)(2,1)S(1)} %collective-permute-done.8.refs_5_), channel_id=1, source_target_pairs={{0,4},{1,5},{2,6},{3,7},{4,0},{5,1},{6,2},{7,3},{8,12},{9,13},{10,... | collective-permute-start | bytes 1572872 | tf_op jit(solution)/shard_map/ppermute | solution.py:154
  61.0 16.8 %collective-permute-start.13 = (bf16[512,512]{1,0:T(8,128)(2,1)S(1)}, bf16[512,512]{1,0:T(8,128)(2,1)S(1)}, u32[]{:S(2)}, u32[]{:S(2)}) collective-permute-start(bf16[512,512]{1,0:T(8,128)(2,1)S(1)} %collective-permute-done.12.refs_10_), channel_id=1, source_target_pairs={{0,448},{1,449},{2,450},{3,451},{4,452},{5,453},{6,454},{7,455},{8... | collective-permute-start | bytes 1572872 | tf_op jit(solution)/shard_map/ppermute | solution.py:154
  63.0 19.5 %collective-permute-start.3 = (bf16[512,512]{1,0:T(8,128)(2,1)S(1)}, bf16[512,512]{1,0:T(8,128)(2,1)S(1)}, u32[]{:S(2)}, u32[]{:S(2)}) collective-permute-start(bf16[512,512]{1,0:T(8,128)(2,1)S(1)} %collective-permute-done.2.refs_12_), channel_id=1, source_target_pairs={{0,64},{1,65},{2,66},{3,67},{4,68},{5,69},{6,70},{7,71},{8,72},{9,... | collective-permute-start | bytes 1572872 | tf_op jit(solution)/shard_map/ppermute | solution.py:154
  83.9 12.3 %collective-permute-start.14 = (f32[768,128]{1,0:T(8,128)S(1)}, f32[768,128]{1,0:T(8,128)S(1)}, u32[]{:S(2)}, u32[]{:S(2)}) collective-permute-start(f32[768,128]{1,0:T(8,128)S(1)} %shard_map.47), channel_id=1, source_target_pairs={{0,1},{1,0},{2,3},{3,2},{4,5},{5,4},{6,7},{7,6},{8,9},{9,8},{10,11... | collective-permute-start | bytes 1179656 | tf_op jit(solution)/shard_map/ppermute | solution.py:154
